TPU v7x, 512 devices: a whole 4x4x16 slice. The times are simulated.
512 devices in a mesh: segment: 64 (over y, x, z_hi, core), fsdp: 8 (over z_lo).
Axes of the slice: x: 4, y: 4, z: 16 (z_hi: 2, z_lo: 8; z = z_hi * 8 + z_lo), core: 2. Of those that a mesh axis runs over, the one named last changes fastest.
Arguments:
- stream: bfloat16 [2, 64, 512, 4096], P(None, 'segment', 'fsdp'), may hold values from -60 to 60
- gain: bfloat16 [2, 64, 4096], P(None, 'segment'), may hold values from 0.099609375 to 1.8984375
- w_query: bfloat16 [2, 64, 32, 128, 128], P(None, 'segment', 'fsdp'), may hold values from -20 to 20
- w_key: bfloat16 [2, 64, 32, 128, 128], P(None, 'segment', 'fsdp'), may hold values from -20 to 20
- w_value: bfloat16 [2, 64, 32, 128, 128], P(None, 'segment', 'fsdp'), may hold values from -0.5 to 0.5
- w_mix: bfloat16 [2, 64, 128, 32, 32], P(None, 'segment', 'fsdp'), may hold values from -1 to 1
- active: int32 [2, 64], P(None, 'segment'), may hold values from 0 to 1
- random_blocks: int32 [2, 64, 8, 2], P(None, 'segment'), may hold values from 0 to 7
Outputs:
- advanced: bfloat16 [2, 64, 512, 4096], P(None, 'segment', 'fsdp')
All inputs are finite; a program needn't handle non-finite values.
Results may differ from a plain program's by a relative error of at most 0.009.
Values may be sent and summed in bfloat16 or wider, within the bound.
No kernel may reach another device: no remote copies, remote signals or barrier semaphores. Data moves between devices by JAX's collectives and lax.ppermute only.
A program may use at most 64 MiB of HBM per device.

v0:
```python
import jax
import jax.numpy as jnp
from jax import lax
from jax.sharding import PartitionSpec as P

BLK = 64
ROUNDS = 2
EPS = 1e-05


def shifted(value, axis, by):
    devices = lax.axis_size(axis)
    return lax.ppermute(value, axis, [(i, (i + by) % devices) for i in range(devices)])


def block_attention(query, keys, values, random_ids):
    heads, seq_len, head_width = query.shape
    count = seq_len // BLK
    query_blocks = query.reshape(heads, count, BLK, head_width)
    key_blocks = keys.reshape(heads, count, BLK, head_width)
    value_blocks = values.reshape(heads, count, BLK, head_width)
    block_ids = jnp.arange(count, dtype=jnp.int32)
    window = jnp.stack(
        [(block_ids - 1) % count, block_ids, (block_ids + 1) % count, jnp.zeros_like(block_ids)],
        axis=1,
    )
    chosen = jnp.concatenate([window, random_ids], axis=1)
    picked_keys = key_blocks[:, chosen].reshape(heads, count, chosen.shape[1] * BLK, head_width)
    picked_values = value_blocks[:, chosen].reshape(heads, count, chosen.shape[1] * BLK, head_width)
    scores = jnp.einsum(
        "hnqd,hnkd->hnqk", query_blocks, picked_keys, preferred_element_type=jnp.float32
    )
    row_max = jnp.max(scores, axis=-1, keepdims=True)
    powers = jnp.exp(scores - row_max)
    weights = (powers / jnp.sum(powers, axis=-1, keepdims=True)).astype(jnp.bfloat16)
    mixed = jnp.einsum(
        "hnqk,hnkd->hnqd", weights, picked_values, preferred_element_type=jnp.float32
    ).astype(jnp.bfloat16)
    return mixed.reshape(heads, seq_len, head_width)


def head_attention(view, queries_w, keys_w, values_w, random_ids):

    def one_segment(items):
        rows, weight_q, weight_k, weight_v, ids = items
        raw = jnp.einsum("thc,hcd->htd", rows, weight_q, preferred_element_type=jnp.float32)
        query = (raw * rows.shape[-1] ** (-0.5)).astype(jnp.bfloat16)
        keys = jnp.einsum(
            "thc,hcd->htd", rows, weight_k, preferred_element_type=jnp.float32
        ).astype(jnp.bfloat16)
        values = jnp.einsum(
            "thc,hcd->htd", rows, weight_v, preferred_element_type=jnp.float32
        ).astype(jnp.bfloat16)
        return block_attention(query, keys, values, ids)

    return lax.map(one_segment, (view, queries_w, keys_w, values_w, random_ids))


def mix_heads(attended, mix_w):
    return jnp.einsum(
        "vhtc,vchg->vtgc",
        attended,
        lax.all_gather(mix_w, "fsdp", axis=1, tiled=True),
        preferred_element_type=jnp.float32,
    ).astype(jnp.bfloat16)


def cycle(values):
    moved = shifted(values, "segment", 1)
    return jnp.where(lax.axis_index("segment") == 0, jnp.roll(moved, 1, axis=0), moved)


def token_layer(state, params):
    queries_w, keys_w, values_w, mix_w, gains, live, random_ids = params
    wide = state.astype(jnp.float32)
    mean_sq = jnp.mean(wide * wide, axis=2, keepdims=True)
    normed = (wide * lax.rsqrt(mean_sq + EPS) * gains[:, None, :].astype(jnp.float32)).astype(
        jnp.bfloat16
    )
    view = normed.reshape(state.shape[0], state.shape[1], -1, queries_w.shape[-1])
    gathered = lax.all_to_all(view, "fsdp", split_axis=2, concat_axis=1, tiled=True)
    attended = head_attention(gathered, queries_w, keys_w, values_w, random_ids)
    returned = lax.all_to_all(attended, "fsdp", split_axis=2, concat_axis=1, tiled=True)
    mixed = mix_heads(returned, mix_w)
    updated = (wide + mixed.reshape(wide.shape).astype(jnp.float32)).astype(jnp.bfloat16)
    return jnp.where(live[:, None, None] > 0, updated, state)


def shards(stream, gain, w_query, w_key, w_value, w_mix, active, random_blocks):
    params = (
        w_query[:, 0],
        w_key[:, 0],
        w_value[:, 0],
        w_mix[:, 0],
        gain[:, 0],
        active[:, 0],
        random_blocks[:, 0],
    )
    state = stream[:, 0]
    for round_index in range(ROUNDS):
        state = token_layer(state, params)
        state = cycle(state)
    return state[:, None]


def solution(mesh):
    in_specs = (
        P(None, "segment", "fsdp", None),
        P(None, "segment", None),
        P(None, "segment", "fsdp", None, None),
        P(None, "segment", "fsdp", None, None),
        P(None, "segment", "fsdp", None, None),
        P(None, "segment", "fsdp", None, None),
        P(None, "segment"),
        P(None, "segment", None, None),
    )
    out_specs = P(None, "segment", "fsdp", None)
    return jax.shard_map(shards, mesh=mesh, in_specs=in_specs, out_specs=out_specs, check_vma=False)
```

profile of v0, /device:TPU:32, one launch (start us, length us, event | category | flops | bytes accessed | tf_op | source)
XLA Modules:
  0.0 546.5 jit_solution(105183954423557872)
XLA Ops:
  5.5 12.8 %all-to-all-start = ((bf16[2,64,32,128]{3,1,0,2:T(8,128)(2,1)}), bf16[2,64,32,128]{3,1,0,2:T(8,128)(2,1)S(1)}, u32[]{:S(2)}, u32[]{:S(2)}) async-start(bf16[2,64,32,128]{3,1,0,2:T(8,128)(2,1)} %copy.69), calls=%async_computation | async-start | bytes 2097152 | tf_op jit(solution)/shard_map/all_to_all | solution.py:81
  18.3 48.3 %all-to-all-done = bf16[2,64,32,128]{3,1,0,2:T(8,128)(2,1)S(1)} async-done(((bf16[2,64,32,128]{3,1,0,2:T(8,128)(2,1)}), bf16[2,64,32,128]{3,1,0,2:T(8,128)(2,1)S(1)}, u32[]{:S(2)}, u32[]{:S(2)}) %all-to-all-start) | async-done | bytes 1048608 | tf_op jit(solution)/shard_map/all_to_all | solution.py:81
  68.9 56.5 %while.24 = (s32[]{:T(128)}, bf16[2,4,512,128]{3,1,0,2:T(4,128)(2,1)}, bf16[2,512,4,128]{3,1,2,0:T(8,128)(2,1)}, bf16[2,4,128,128]{3,2,1,0:T(8,128)(2,1)S(1)}, b...) while((s32[]{:T(128)}, ...), condition=%wide.region_4.5_spmd, body=%wide.region_1.4_spmd.sunk | while | flops 609226816 | bytes 59140032 | solution.py:56
  73.3 2.9 copy.106
  87.6 7.3 %fusion.139 = bf16[4,8,64,128]{3,2,1,0:T(8,128)(2,1)} fusion(bf16[4,8,384,128]{3,2,1,0:T(8,128)(2,1)S(1)} %bitcast.258, f32[4,8,64]{2,1,0:T(8,128)S(1)} %fusion.138, f32[4,8,64,384]{3,2,1,0:T(8,128)} %copy-done), kind=kOutput, calls=%fused_computation.9.clone.1 | convolution fusion | flops 203950464 | bytes 6823936 | tf_op jit(solution)/shard_map/while/body/eval_jaxpr/hnqk,hnkd->hnqd/dot_general | solution.py:36
  101.5 2.9 copy.106
  115.9 7.3 %fusion.139 = bf16[4,8,64,128]{3,2,1,0:T(8,128)(2,1)} fusion(bf16[4,8,384,128]{3,2,1,0:T(8,128)(2,1)S(1)} %bitcast.258, f32[4,8,64]{2,1,0:T(8,128)S(1)} %fusion.138, f32[4,8,64,384]{3,2,1,0:T(8,128)} %copy-done), kind=kOutput, calls=%fused_computation.9.clone.1 | convolution fusion | flops 203950464 | bytes 6823936 | tf_op jit(solution)/shard_map/while/body/eval_jaxpr/hnqk,hnkd->hnqd/dot_general | solution.py:36
  125.4 7.2 %all-to-all-start.1 = ((bf16[2,4,512,128]{3,1,0,2:T(4,128)(2,1)}), bf16[2,4,512,128]{3,1,0,2:T(4,128)(2,1)S(1)}, u32[]{:S(2)}, u32[]{:S(2)}) async-start(bf16[2,4,512,128]{3,1,0,2:T(4,128)(2,1)} %get-tuple-element.187), calls=%async_computation.1 | async-start | bytes 2097152 | tf_op jit(solution)/shard_map/all_to_all | solution.py:83
  134.4 89.3 %all-gather = bf16[2,1,128,32,32]{3,4,2,0,1:T(8,128)(2,1)S(1)} all-gather(bf16[2,1,16,32,32]{3,4,2,0,1:T(8,128)(2,1)} %copy.74), channel_id=2, replica_groups=mesh['segment'=64,'fsdp'=8] {'fsdp'}, dimensions={2}, use_global_device_ids=true | all-gather | bytes 589824 | tf_op jit(solution)/shard_map/all_gather | solution.py:63
  223.7 3.3 copy.73
  227.0 4.2 convert_bitcast_fusion.1
  231.2 5.3 copy.75
  241.7 51.0 %collective-permute-done = bf16[2,64,4096]{2,1,0:T(8,128)(2,1)S(1)} collective-permute-done((bf16[2,64,4096]{2,1,0:T(8,128)(2,1)}, bf16[2,64,4096]{2,1,0:T(8,128)(2,1)S(1)}, u32[]{:S(2)}, u32[]{:S(2)}) %collective-permute-start) | collective-permute-done | bytes 1048608 | tf_op jit(solution)/shard_map/ppermute | solution.py:13
  295.6 19.6 %all-to-all-start.2 = ((bf16[2,64,32,128]{3,1,0,2:T(8,128)(2,1)}), bf16[2,64,32,128]{3,1,0,2:T(8,128)(2,1)S(1)}, u32[]{:S(2)}, u32[]{:S(2)}) async-start(bf16[2,64,32,128]{3,1,0,2:T(8,128)(2,1)} %copy_bitcast_fusion), calls=%async_computation.2 | async-start | bytes 2097152 | tf_op jit(solution)/shard_map/all_to_all | solution.py:81
  315.2 38.3 %all-to-all-done.2 = bf16[2,64,32,128]{3,1,0,2:T(8,128)(2,1)S(1)} async-done(((bf16[2,64,32,128]{3,1,0,2:T(8,128)(2,1)}), bf16[2,64,32,128]{3,1,0,2:T(8,128)(2,1)S(1)}, u32[]{:S(2)}, u32[]{:S(2)}) %all-to-all-start.2) | async-done | bytes 1048608 | tf_op jit(solution)/shard_map/all_to_all | solution.py:81
  355.8 56.6 %while.25 = (s32[]{:T(128)}, bf16[2,4,512,128]{3,1,0,2:T(4,128)(2,1)}, bf16[2,512,4,128]{3,1,2,0:T(8,128)(2,1)}, bf16[2,4,128,128]{3,2,1,0:T(8,128)(2,1)S(1)}, b...) while((s32[]{:T(128)}, ...), condition=%wide.region_9.10_spmd, body=%wide.region_6.9_spmd.sunk | while | flops 609226816 | bytes 59140032 | solution.py:56
  360.1 2.9 copy.110
  374.5 7.3 %fusion.156 = bf16[4,8,64,128]{3,2,1,0:T(8,128)(2,1)} fusion(bf16[4,8,384,128]{3,2,1,0:T(8,128)(2,1)S(1)} %bitcast.259, f32[4,8,64]{2,1,0:T(8,128)S(1)} %fusion.155, f32[4,8,64,384]{3,2,1,0:T(8,128)} %copy-done.1), kind=kOutput, calls=%fused_computation.49.clone.1 | convolution fusion | flops 203950464 | bytes 6823936 | tf_op jit(solution)/shard_map/while/body/eval_jaxpr/hnqk,hnkd->hnqd/dot_general | solution.py:36
  402.8 7.3 %fusion.156 = bf16[4,8,64,128]{3,2,1,0:T(8,128)(2,1)} fusion(bf16[4,8,384,128]{3,2,1,0:T(8,128)(2,1)S(1)} %bitcast.259, f32[4,8,64]{2,1,0:T(8,128)S(1)} %fusion.155, f32[4,8,64,384]{3,2,1,0:T(8,128)} %copy-done.1), kind=kOutput, calls=%fused_computation.49.clone.1 | convolution fusion | flops 203950464 | bytes 6823936 | tf_op jit(solution)/shard_map/while/body/eval_jaxpr/hnqk,hnkd->hnqd/dot_general | solution.py:36
  412.4 55.1 %all_to_all.72 = bf16[2,4,512,128]{3,1,0,2:T(4,128)(2,1)S(1)} all-to-all(bf16[2,4,512,128]{3,1,0,2:T(4,128)(2,1)} %get-tuple-element.188), channel_id=1, replica_groups=mesh['segment'=64,'fsdp'=8] {'fsdp'}, dimensions={2} | all-to-all | bytes 2097152 | tf_op jit(solution)/shard_map/all_to_all | solution.py:83
  467.5 3.2 copy.79
  470.7 4.2 convert_bitcast_fusion
  474.9 4.5 copy.80
  484.9 60.4 %collective-permute-done.1 = bf16[2,64,4096]{2,1,0:T(8,128)(2,1)S(1)} collective-permute-done((bf16[2,64,4096]{2,1,0:T(8,128)(2,1)S(1)}, bf16[2,64,4096]{2,1,0:T(8,128)(2,1)S(1)}, u32[]{:S(2)}, u32[]{:S(2)}) %collective-permute-start.1) | collective-permute-done | bytes 1048608 | tf_op jit(solution)/shard_map/ppermute | solution.py:13
  (123 shorter events, 101.5 us)
Async XLA Ops:
  5.5 63.4 %copy-start.7 = (bf16[2,1,4,128,128]{4,3,2,1,0:T(8,128)(2,1)S(1)}, bf16[2,1,4,128,128]{4,3,2,1,0:T(8,128)(2,1)}, u32[]{:S(2)}) copy-start(bf16[2,1,4,128,128]{4,3,2,1,0:T(8,128)(2,1)} %param.14) | copy-start | bytes 786436
  5.5 63.4 %copy-start.8 = (s32[2,1,8,2]{2,3,1,0:T(2,128)S(1)}, s32[2,1,8,2]{2,3,1,0:T(2,128)}, u32[]{:S(2)}) copy-start(s32[2,1,8,2]{2,3,1,0:T(2,128)} %param.19) | copy-start | bytes 388
  5.5 61.1 %all-to-all-start = ((bf16[2,64,32,128]{3,1,0,2:T(8,128)(2,1)}), bf16[2,64,32,128]{3,1,0,2:T(8,128)(2,1)S(1)}, u32[]{:S(2)}, u32[]{:S(2)}) async-start(bf16[2,64,32,128]{3,1,0,2:T(8,128)(2,1)} %copy.69), calls=%async_computation | async-start | bytes 2097152 | tf_op jit(solution)/shard_map/all_to_all | solution.py:81
  68.9 65.4 %copy-start.9 = (s32[2,1]{0,1:T(1,128)S(1)}, s32[2,1]{0,1:T(1,128)}, u32[]{:S(2)}) copy-start(s32[2,1]{0,1:T(1,128)} %param.18) | copy-start | bytes 28
  79.0 1.7 copy-start
  107.3 1.7 copy-start
  125.4 98.2 %all-to-all-start.1 = ((bf16[2,4,512,128]{3,1,0,2:T(4,128)(2,1)}), bf16[2,4,512,128]{3,1,0,2:T(4,128)(2,1)S(1)}, u32[]{:S(2)}, u32[]{:S(2)}) async-start(bf16[2,4,512,128]{3,1,0,2:T(4,128)(2,1)} %get-tuple-element.187), calls=%async_computation.1 | async-start | bytes 2097152 | tf_op jit(solution)/shard_map/all_to_all | solution.py:83
  223.7 7.6 %copy-start.2 = (bf16[2,1,128,32,32]{3,4,2,0,1:T(8,128)(2,1)}, bf16[2,1,128,32,32]{3,4,2,0,1:T(8,128)(2,1)S(1)}, u32[]{:S(2)}) copy-start(bf16[2,1,128,32,32]{3,4,2,0,1:T(8,128)(2,1)S(1)} %all-gather) | copy-start | bytes 1572868
  236.5 1.9 copy-start.4
  239.8 52.9 %collective-permute-start = (bf16[2,64,4096]{2,1,0:T(8,128)(2,1)}, bf16[2,64,4096]{2,1,0:T(8,128)(2,1)S(1)}, u32[]{:S(2)}, u32[]{:S(2)}) collective-permute-start(bf16[2,64,4096]{2,1,0:T(8,128)(2,1)} %fusion.67), channel_id=1, source_target_pairs={{0,8},{8,16},{16,24},{24,32},{32,40},{40,48},{48,56},{56,64},{64,7... | collective-permute-start | bytes 3145736 | tf_op jit(solution)/shard_map/ppermute | solution.py:13
  293.2 1.0 copy-start.5
  295.6 57.8 %all-to-all-start.2 = ((bf16[2,64,32,128]{3,1,0,2:T(8,128)(2,1)}), bf16[2,64,32,128]{3,1,0,2:T(8,128)(2,1)S(1)}, u32[]{:S(2)}, u32[]{:S(2)}) async-start(bf16[2,64,32,128]{3,1,0,2:T(8,128)(2,1)} %copy_bitcast_fusion), calls=%async_computation.2 | async-start | bytes 2097152 | tf_op jit(solution)/shard_map/all_to_all | solution.py:81
  365.9 1.7 copy-start.1
  394.2 1.7 copy-start.1
  412.4 58.3 %copy-start.3 = (bf16[2,1,128,32,32]{3,4,2,0,1:T(8,128)(2,1)S(1)}, bf16[2,1,128,32,32]{3,4,2,0,1:T(8,128)(2,1)}, u32[]{:S(2)}) copy-start(bf16[2,1,128,32,32]{3,4,2,0,1:T(8,128)(2,1)} %copy-done.2) | copy-start | bytes 1572868
  479.4 1.6 copy-start.6
  483.0 62.3 %collective-permute-start.1 = (bf16[2,64,4096]{2,1,0:T(8,128)(2,1)S(1)}, bf16[2,64,4096]{2,1,0:T(8,128)(2,1)S(1)}, u32[]{:S(2)}, u32[]{:S(2)}) collective-permute-start(bf16[2,64,4096]{2,1,0:T(8,128)(2,1)S(1)} %fusion.66), channel_id=1, source_target_pairs={{0,8},{8,16},{16,24},{24,32},{32,40},{40,48},{48,56},{56,64},{64,7... | collective-permute-start | bytes 3145736 | tf_op jit(solution)/shard_map/ppermute | solution.py:13
where the time goes:
time: 548 us; the launch traced here: 547 us
  waiting for transfers between devices  198 us (36%)
  blocking collectives  144 us (26%)
  local copies, waits for them, and re-layouts  85.7 us (16%)
  matrix products  59.8 us (11%)
  starting transfers between devices  43.3 us (8%)
  other arithmetic  14.7 us (3%)
    ppermute x2, waiting for transfers between devices, shifted(): lax.ppermute(value, axis, [(i, (i + by) % devices) for i in range(devices)])  111 us
    all_gather x1, blocking collectives, mix_heads(): lax.all_gather(mix_w, 'fsdp', axis=1, tiled=True)  89.3 us
    all_to_all x2, waiting for transfers between devices, token_layer(): lax.all_to_all(view, 'fsdp', split_axis=2, concat_axis=1, tiled=True)  86.6 us
    all_to_all x1, blocking collectives, token_layer(): lax.all_to_all(attended, 'fsdp', split_axis=2, concat_axis=1, tiled=True)  55.1 us
    all_to_all x2, starting transfers between devices, token_layer(): lax.all_to_all(view, 'fsdp', split_axis=2, concat_axis=1, tiled=True)  32.4 us
    dot_general x4, matrix products, block_attention(): jnp.einsum('hnqk,hnkd->hnqd', weights, picked_values, preferred_element_t...  29.3 us
    gather x8, local copies, waits for them, and re-layouts, block_attention(): value_blocks[:, chosen]  22.4 us
    gather x8, local copies, waits for them, and re-layouts, block_attention(): key_blocks[:, chosen]  22.3 us
  transfers between devices with their start and end apart: 5, of which 4 were waited for; matrix products, arithmetic and copies ran while one was open for 0% of the time, Pallas kernels for 0%

commit v1 on v0

--- a/solution.py
+++ b/solution.py
@@ -80,7 +80,10 @@
     view = normed.reshape(state.shape[0], state.shape[1], -1, queries_w.shape[-1])
     gathered = lax.all_to_all(view, "fsdp", split_axis=2, concat_axis=1, tiled=True)
     attended = head_attention(gathered, queries_w, keys_w, values_w, random_ids)
-    returned = lax.all_to_all(attended, "fsdp", split_axis=2, concat_axis=1, tiled=True)
+    returned = jnp.concatenate(
+        lax.all_to_all(jnp.stack(jnp.split(attended, lax.axis_size("fsdp"), axis=2)), "fsdp", 0, 0),
+        axis=1,
+    )
     mixed = mix_heads(returned, mix_w)
     updated = (wide + mixed.reshape(wide.shape).astype(jnp.float32)).astype(jnp.bfloat16)
     return jnp.where(live[:, None, None] > 0, updated, state)

time: 548 us -> 566 us (1.033)
  local copies, waits for them, and re-layouts: 85.7 us -> 103 us
    unnamed x19 -> x35, local copies, waits for them, and re-layouts: 4.28 us -> 20.9 us
    all_to_all x2 -> x0, local copies, waits for them, and re-layouts: 6.55 us -> none  [token_layer(): lax.all_to_all(attended, 'fsdp', split_axis=2, concat_axis=1, tiled=True)]
    reshape x0 -> x2, local copies, waits for them, and re-layouts: none -> 6.19 us  [token_layer(): jnp.concatenate(lax.all_to_all(jnp.stack(jnp.split(attended, lax.axis_siz...]
where the time goes in v1:
time: 566 us; the launch traced here: 564 us
  waiting for transfers between devices  198 us (35%)
  blocking collectives  145 us (26%)
  local copies, waits for them, and re-layouts  103 us (18%)
  matrix products  59.8 us (11%)
  starting transfers between devices  43.3 us (8%)
  other arithmetic  14.7 us (3%)
    ppermute x2, waiting for transfers between devices, shifted(): lax.ppermute(value, axis, [(i, (i + by) % devices) for i in range(devices)])  111 us
    all_gather x1, blocking collectives, mix_heads(): lax.all_gather(mix_w, 'fsdp', axis=1, tiled=True)  90.2 us
    all_to_all x2, waiting for transfers between devices, token_layer(): lax.all_to_all(view, 'fsdp', split_axis=2, concat_axis=1, tiled=True)  86.6 us
    all_to_all x1, blocking collectives, token_layer(): lax.all_to_all(jnp.stack(jnp.split(attended, lax.axis_size('fsdp'), axis=...  54.8 us
    all_to_all x2, starting transfers between devices, token_layer(): lax.all_to_all(view, 'fsdp', split_axis=2, concat_axis=1, tiled=True)  32.4 us
    dot_general x4, matrix products, block_attention(): jnp.einsum('hnqk,hnkd->hnqd', weights, picked_values, preferred_element_t...  29.2 us
    gather x8, local copies, waits for them, and re-layouts, block_attention(): value_blocks[:, chosen]  22.4 us
    gather x8, local copies, waits for them, and re-layouts, block_attention(): key_blocks[:, chosen]  22.3 us
  transfers between devices with their start and end apart: 5, of which 4 were waited for; matrix products, arithmetic and copies ran while one was open for 0% of the time, Pallas kernels for 0%

profile of v1, /device:TPU:32, one launch (start us, length us, event | category | flops | bytes accessed | tf_op | source)
XLA Modules:
  0.0 563.9 jit_solution(13023628430575466286)
XLA Ops:
  5.5 12.8 %all-to-all-start = ((bf16[2,64,32,128]{3,1,0,2:T(8,128)(2,1)}), bf16[2,64,32,128]{3,1,0,2:T(8,128)(2,1)S(1)}, u32[]{:S(2)}, u32[]{:S(2)}) async-start(bf16[2,64,32,128]{3,1,0,2:T(8,128)(2,1)} %copy.69), calls=%async_computation | async-start | bytes 2097152 | tf_op jit(solution)/shard_map/all_to_all | solution.py:81
  18.3 48.3 %all-to-all-done = bf16[2,64,32,128]{3,1,0,2:T(8,128)(2,1)S(1)} async-done(((bf16[2,64,32,128]{3,1,0,2:T(8,128)(2,1)}), bf16[2,64,32,128]{3,1,0,2:T(8,128)(2,1)S(1)}, u32[]{:S(2)}, u32[]{:S(2)}) %all-to-all-start) | async-done | bytes 1048608 | tf_op jit(solution)/shard_map/all_to_all | solution.py:81
  68.8 55.7 %while.24 = (s32[]{:T(128)}, bf16[2,4,512,128]{3,2,1,0:T(8,128)(2,1)}, bf16[2,512,4,128]{3,1,2,0:T(8,128)(2,1)}, bf16[2,4,128,128]{3,2,1,0:T(8,128)(2,1)S(1)}, b...) while((s32[]{:T(128)}, ...), condition=%wide.region_4.5_spmd, body=%wide.region_1.4_spmd.sunk | while | flops 609226816 | bytes 59140032 | solution.py:56
  73.1 2.9 copy.95
  87.5 7.3 %fusion.139 = bf16[4,8,64,128]{3,2,1,0:T(8,128)(2,1)} fusion(bf16[4,8,384,128]{3,2,1,0:T(8,128)(2,1)S(1)} %bitcast.286, f32[4,8,64]{2,1,0:T(8,128)S(1)} %fusion.138, f32[4,8,64,384]{3,2,1,0:T(8,128)} %copy-done), kind=kOutput, calls=%fused_computation.9.clone.1 | convolution fusion | flops 203950464 | bytes 6823936 | tf_op jit(solution)/shard_map/while/body/eval_jaxpr/hnqk,hnkd->hnqd/dot_general | solution.py:36
  101.0 2.9 copy.95
  115.3 7.3 %fusion.139 = bf16[4,8,64,128]{3,2,1,0:T(8,128)(2,1)} fusion(bf16[4,8,384,128]{3,2,1,0:T(8,128)(2,1)S(1)} %bitcast.286, f32[4,8,64]{2,1,0:T(8,128)S(1)} %fusion.138, f32[4,8,64,384]{3,2,1,0:T(8,128)} %copy-done), kind=kOutput, calls=%fused_computation.9.clone.1 | convolution fusion | flops 203950464 | bytes 6823936 | tf_op jit(solution)/shard_map/while/body/eval_jaxpr/hnqk,hnkd->hnqd/dot_general | solution.py:36
  137.0 7.2 %all-to-all-start.1 = ((bf16[8,2,4,64,128]{4,3,2,1,0:T(8,128)(2,1)}), bf16[8,2,4,64,128]{4,3,2,1,0:T(8,128)(2,1)S(1)}, u32[]{:S(2)}, u32[]{:S(2)}) async-start(bf16[8,2,4,64,128]{4,3,2,1,0:T(8,128)(2,1)} %bitcast_dynamic-update-slice_fusion.8), calls=%async_computation.1 | async-start | bytes 2097152 | tf_op jit(solution)/shard_map/all_to_all | solution.py:84
  145.0 90.2 %all-gather = bf16[2,1,128,32,32]{3,4,2,0,1:T(8,128)(2,1)S(1)} all-gather(bf16[2,1,16,32,32]{3,4,2,0,1:T(8,128)(2,1)} %copy.73), channel_id=2, replica_groups=mesh['segment'=64,'fsdp'=8] {'fsdp'}, dimensions={2}, use_global_device_ids=true | all-gather | bytes 589824 | tf_op jit(solution)/shard_map/all_gather | solution.py:63
  235.2 3.2 copy.72
  238.5 4.2 convert_bitcast_fusion.1
  242.7 5.3 copy.74
  253.1 51.0 %collective-permute-done = bf16[2,64,4096]{2,1,0:T(8,128)(2,1)S(1)} collective-permute-done((bf16[2,64,4096]{2,1,0:T(8,128)(2,1)}, bf16[2,64,4096]{2,1,0:T(8,128)(2,1)S(1)}, u32[]{:S(2)}, u32[]{:S(2)}) %collective-permute-start) | collective-permute-done | bytes 1048608 | tf_op jit(solution)/shard_map/ppermute | solution.py:13
  307.0 19.6 %all-to-all-start.2 = ((bf16[2,64,32,128]{3,1,0,2:T(8,128)(2,1)}), bf16[2,64,32,128]{3,1,0,2:T(8,128)(2,1)S(1)}, u32[]{:S(2)}, u32[]{:S(2)}) async-start(bf16[2,64,32,128]{3,1,0,2:T(8,128)(2,1)} %copy_bitcast_fusion), calls=%async_computation.2 | async-start | bytes 2097152 | tf_op jit(solution)/shard_map/all_to_all | solution.py:81
  326.6 38.2 %all-to-all-done.2 = bf16[2,64,32,128]{3,1,0,2:T(8,128)(2,1)S(1)} async-done(((bf16[2,64,32,128]{3,1,0,2:T(8,128)(2,1)}), bf16[2,64,32,128]{3,1,0,2:T(8,128)(2,1)S(1)}, u32[]{:S(2)}, u32[]{:S(2)}) %all-to-all-start.2) | async-done | bytes 1048608 | tf_op jit(solution)/shard_map/all_to_all | solution.py:81
  367.1 55.6 %while.25 = (s32[]{:T(128)}, bf16[2,4,512,128]{3,2,1,0:T(8,128)(2,1)}, bf16[2,512,4,128]{3,1,2,0:T(8,128)(2,1)}, bf16[2,4,128,128]{3,2,1,0:T(8,128)(2,1)S(1)}, b...) while((s32[]{:T(128)}, ...), condition=%wide.region_9.10_spmd, body=%wide.region_6.9_spmd.sunk | while | flops 609226816 | bytes 59140032 | solution.py:56
  371.4 2.9 copy.98
  385.8 7.3 %fusion.156 = bf16[4,8,64,128]{3,2,1,0:T(8,128)(2,1)} fusion(bf16[4,8,384,128]{3,2,1,0:T(8,128)(2,1)S(1)} %bitcast.287, f32[4,8,64]{2,1,0:T(8,128)S(1)} %fusion.155, f32[4,8,64,384]{3,2,1,0:T(8,128)} %copy-done.1), kind=kOutput, calls=%fused_computation.49.clone.1 | convolution fusion | flops 203950464 | bytes 6823936 | tf_op jit(solution)/shard_map/while/body/eval_jaxpr/hnqk,hnkd->hnqd/dot_general | solution.py:36
  413.6 7.3 %fusion.156 = bf16[4,8,64,128]{3,2,1,0:T(8,128)(2,1)} fusion(bf16[4,8,384,128]{3,2,1,0:T(8,128)(2,1)S(1)} %bitcast.287, f32[4,8,64]{2,1,0:T(8,128)S(1)} %fusion.155, f32[4,8,64,384]{3,2,1,0:T(8,128)} %copy-done.1), kind=kOutput, calls=%fused_computation.49.clone.1 | convolution fusion | flops 203950464 | bytes 6823936 | tf_op jit(solution)/shard_map/while/body/eval_jaxpr/hnqk,hnkd->hnqd/dot_general | solution.py:36
  430.4 54.8 %all_to_all.46 = bf16[8,2,4,64,128]{4,3,2,1,0:T(8,128)(2,1)S(1)} all-to-all(bf16[8,2,4,64,128]{4,3,2,1,0:T(8,128)(2,1)S(1)} %bitcast_dynamic-update-slice_fusion), channel_id=1, replica_groups=mesh['segment'=64,'fsdp'=8] {'fsdp'}, dimensions={0} | all-to-all | bytes 2097152 | tf_op jit(solution)/shard_map/all_to_all | solution.py:84
  485.1 3.0 copy.77
  488.1 4.2 convert_bitcast_fusion
  492.3 4.5 copy.78
  502.3 60.4 %collective-permute-done.1 = bf16[2,64,4096]{2,1,0:T(8,128)(2,1)S(1)} collective-permute-done((bf16[2,64,4096]{2,1,0:T(8,128)(2,1)S(1)}, bf16[2,64,4096]{2,1,0:T(8,128)(2,1)S(1)}, u32[]{:S(2)}, u32[]{:S(2)}) %collective-permute-start.1) | collective-permute-done | bytes 1048608 | tf_op jit(solution)/shard_map/ppermute | solution.py:13
  (141 shorter events, 118.6 us)
Async XLA Ops:
  5.5 63.3 %copy-start.7 = (bf16[2,1,4,128,128]{4,3,2,1,0:T(8,128)(2,1)S(1)}, bf16[2,1,4,128,128]{4,3,2,1,0:T(8,128)(2,1)}, u32[]{:S(2)}) copy-start(bf16[2,1,4,128,128]{4,3,2,1,0:T(8,128)(2,1)} %param.14) | copy-start | bytes 786436
  5.5 63.3 %copy-start.9 = (s32[2,1,8,2]{2,3,1,0:T(2,128)S(1)}, s32[2,1,8,2]{2,3,1,0:T(2,128)}, u32[]{:S(2)}) copy-start(s32[2,1,8,2]{2,3,1,0:T(2,128)} %param.19) | copy-start | bytes 388
  5.5 61.1 %all-to-all-start = ((bf16[2,64,32,128]{3,1,0,2:T(8,128)(2,1)}), bf16[2,64,32,128]{3,1,0,2:T(8,128)(2,1)S(1)}, u32[]{:S(2)}, u32[]{:S(2)}) async-start(bf16[2,64,32,128]{3,1,0,2:T(8,128)(2,1)} %copy.69), calls=%async_computation | async-start | bytes 2097152 | tf_op jit(solution)/shard_map/all_to_all | solution.py:81
  78.9 1.6 copy-start
  106.7 1.6 copy-start
  124.5 19.7 %copy-start.8 = (bf16[2,1,16,32,32]{4,3,2,1,0:T(8,128)(2,1)S(1)}, bf16[2,1,16,32,32]{4,3,2,1,0:T(8,128)(2,1)}, u32[]{:S(2)}) copy-start(bf16[2,1,16,32,32]{4,3,2,1,0:T(8,128)(2,1)} %param.17) | copy-start | bytes 196612
  124.5 20.5 %copy-start.10 = (s32[2,1]{0,1:T(1,128)S(1)}, s32[2,1]{0,1:T(1,128)}, u32[]{:S(2)}) copy-start(s32[2,1]{0,1:T(1,128)} %param.18) | copy-start | bytes 28
  137.0 98.2 %all-to-all-start.1 = ((bf16[8,2,4,64,128]{4,3,2,1,0:T(8,128)(2,1)}), bf16[8,2,4,64,128]{4,3,2,1,0:T(8,128)(2,1)S(1)}, u32[]{:S(2)}, u32[]{:S(2)}) async-start(bf16[8,2,4,64,128]{4,3,2,1,0:T(8,128)(2,1)} %bitcast_dynamic-update-slice_fusion.8), calls=%async_computation.1 | async-start | bytes 2097152 | tf_op jit(solution)/shard_map/all_to_all | solution.py:84
  235.2 7.5 %copy-start.2 = (bf16[2,1,128,32,32]{3,4,2,0,1:T(8,128)(2,1)}, bf16[2,1,128,32,32]{3,4,2,0,1:T(8,128)(2,1)S(1)}, u32[]{:S(2)}) copy-start(bf16[2,1,128,32,32]{3,4,2,0,1:T(8,128)(2,1)S(1)} %all-gather) | copy-start | bytes 1572868
  248.0 1.9 copy-start.4
  251.2 52.9 %collective-permute-start = (bf16[2,64,4096]{2,1,0:T(8,128)(2,1)}, bf16[2,64,4096]{2,1,0:T(8,128)(2,1)S(1)}, u32[]{:S(2)}, u32[]{:S(2)}) collective-permute-start(bf16[2,64,4096]{2,1,0:T(8,128)(2,1)} %fusion.67), channel_id=1, source_target_pairs={{0,8},{8,16},{16,24},{24,32},{32,40},{40,48},{48,56},{56,64},{64,7... | collective-permute-start | bytes 3145736 | tf_op jit(solution)/shard_map/ppermute | solution.py:13
  304.7 1.0 copy-start.5
  307.0 57.8 %all-to-all-start.2 = ((bf16[2,64,32,128]{3,1,0,2:T(8,128)(2,1)}), bf16[2,64,32,128]{3,1,0,2:T(8,128)(2,1)S(1)}, u32[]{:S(2)}, u32[]{:S(2)}) async-start(bf16[2,64,32,128]{3,1,0,2:T(8,128)(2,1)} %copy_bitcast_fusion), calls=%async_computation.2 | async-start | bytes 2097152 | tf_op jit(solution)/shard_map/all_to_all | solution.py:81
  377.2 1.6 copy-start.1
  405.0 1.6 copy-start.1
  426.5 61.6 %copy-start.3 = (bf16[2,1,128,32,32]{3,4,2,0,1:T(8,128)(2,1)S(1)}, bf16[2,1,128,32,32]{3,4,2,0,1:T(8,128)(2,1)}, u32[]{:S(2)}) copy-start(bf16[2,1,128,32,32]{3,4,2,0,1:T(8,128)(2,1)} %copy-done.2) | copy-start | bytes 1572868
  496.8 1.6 copy-start.6
  500.3 62.3 %collective-permute-start.1 = (bf16[2,64,4096]{2,1,0:T(8,128)(2,1)S(1)}, bf16[2,64,4096]{2,1,0:T(8,128)(2,1)S(1)}, u32[]{:S(2)}, u32[]{:S(2)}) collective-permute-start(bf16[2,64,4096]{2,1,0:T(8,128)(2,1)S(1)} %fusion.66), channel_id=1, source_target_pairs={{0,8},{8,16},{16,24},{24,32},{32,40},{40,48},{48,56},{56,64},{64,7... | collective-permute-start | bytes 3145736 | tf_op jit(solution)/shard_map/ppermute | solution.py:13
